TPU v7x, 32 devices: a whole 2x2x4 slice. The times are simulated.
32 devices in a mesh: dp: 8 (over y, x, core), tensor: 4 (over z).
Axes of the slice: x: 2, y: 2, z: 4, core: 2. Of those that a mesh axis runs over, the one named last changes fastest.
Arguments:
- block_input: bfloat16 [16384, 768], P(('dp', 'tensor')), may hold values from -6 to 6
- cotangent: bfloat16 [16384, 768], P(('dp', 'tensor')), may hold values from -6 to 6
- segment_ids: int32 [16384], P('dp'), may hold values from 0 to 1, as said below
- pad_mask: int32 [16384], P('dp'), may hold values from 0 to 1, as said below
- w_query: bfloat16 [768, 768], P(None, 'tensor'), may hold values from -0.21875 to 0.21875
- b_query: bfloat16 [768], P('tensor'), may hold values from -1.5 to 1.5
- w_key: bfloat16 [768, 768], P(None, 'tensor'), may hold values from -0.21875 to 0.21875
- w_value: bfloat16 [768, 768], P(None, 'tensor'), may hold values from -0.21875 to 0.21875
- b_value: bfloat16 [768], P('tensor'), may hold values from -1.5 to 1.5
- w_out: bfloat16 [768, 768], P('tensor'), may hold values from -0.875 to 0.875
- b_out: bfloat16 [768], replicated, may hold values from -1.5 to 1.5
- gain_one: bfloat16 [768], replicated, may hold values from 0.25 to 1.75
- shift_one: bfloat16 [768], replicated, may hold values from -1.5 to 1.5
- w_inner: bfloat16 [768, 3072], P(None, 'tensor'), may hold values from -0.21875 to 0.21875
- b_inner: bfloat16 [3072], P('tensor'), may hold values from -1.5 to 1.5
- w_outer: bfloat16 [3072, 768], P('tensor'), may hold values from -0.15625 to 0.15625
- b_outer: bfloat16 [768], replicated, may hold values from -1.5 to 1.5
- gain_two: bfloat16 [768], replicated, may hold values from 0.25 to 1.75
- shift_two: bfloat16 [768], replicated, may hold values from -1.5 to 1.5
Outputs:
- output: bfloat16 [16384, 768], P(('dp', 'tensor'))
- grad_input: float32 [16384, 768], P(('dp', 'tensor'))
- grad_w_query: float32 [768, 768], P(None, 'tensor')
- grad_b_query: float32 [768], P('tensor')
- grad_w_key: float32 [768, 768], P(None, 'tensor')
- grad_w_value: float32 [768, 768], P(None, 'tensor')
- grad_b_value: float32 [768], P('tensor')
- grad_w_out: float32 [768, 768], P('tensor')
- grad_b_out: float32 [768], replicated
- grad_gain_one: float32 [768], replicated
- grad_shift_one: float32 [768], replicated
- grad_w_inner: float32 [768, 3072], P(None, 'tensor')
- grad_b_inner: float32 [3072], P('tensor')
- grad_w_outer: float32 [3072, 768], P('tensor')
- grad_b_outer: float32 [768], replicated
- grad_gain_two: float32 [768], replicated
- grad_shift_two: float32 [768], replicated
Inputs may be any that keep to these rules, and one draw needn't show every extreme that they name: `segment_ids`: tokens form rows of 128 positions; a row holds one sequence with id 0, or two of 64 positions with ids 0 then 1. `pad_mask`: the real tokens of each sequence are its first ones, 4 or more.
All inputs are finite; a program needn't handle non-finite values.
Results may differ from a plain program's by a relative error of at most 0.017.
Values may be sent and summed in bfloat16 or wider, within the bound.
A program may use at most 128 MiB of HBM per device.

v0:
```python
import functools
import math

import jax
import jax.numpy as jnp
from jax import lax
from jax.experimental import pallas as pl
from jax.experimental.pallas import tpu as pltpu
from jax.sharding import PartitionSpec as P

HEAD_DIM = 64
SEQ = 128
EPSILON = 1e-05
MASKED = -1e30
BF = jnp.bfloat16
F32 = jnp.float32
MESH = pl.DeviceIdType.MESH
GROUP = 8


def places():
    dp = lax.axis_index("dp")
    z = lax.axis_index("tensor")
    core = dp % 2
    along_x = (dp // 2) % 2
    along_y = (dp // 4) % 2
    peers = {
        "c": {"dp": dp + 1 - 2 * core, "tensor": z},
        "x": {"dp": dp + 2 - 4 * along_x, "tensor": z},
        "y": {"dp": dp + 4 - 8 * along_y, "tensor": z},
        1: {"dp": dp, "tensor": z + 1 - 2 * (z % 2)},
        2: {"dp": dp, "tensor": (z + 2) % 4},
        3: {"dp": dp, "tensor": 3 - z},
    }
    return dp, z, core, along_x, along_y, peers


def outer_peers(dp, z, outer):
    found = []
    weight = GROUP
    while weight < GROUP * outer:
        bit = (dp // weight) % 2
        found.append({"dp": dp + weight - 2 * weight * bit, "tensor": z})
        weight *= 2
    return found


def greet(peer_list):
    barrier = pltpu.get_barrier_semaphore()
    for peer in peer_list:
        pl.semaphore_signal(barrier, inc=1, device_id=peer, device_id_type=MESH)
    pl.semaphore_wait(barrier, len(peer_list))


def rows(start, size):
    return pl.ds(pl.multiple_of(start, 16), size)


class Spread:
    def __init__(self, block, half, send, recv):
        _, _, core, ax, ay, peers = places()
        base = core * half
        part = half // 2
        quarter = part // 2
        eighth = quarter // 2
        first = base + ax * quarter
        second = base + part + ay * quarter
        self.steps = []
        plan = (
            ((rows(first + ay * eighth, eighth), "y"), (rows(second + ax * eighth, eighth), "x")),
            ((rows(first, quarter), "x"), (rows(second, quarter), "y")),
            ((rows(base, half), "c"),),
        )
        place = 0
        for step in plan:
            copies = []
            for span, name in step:
                copies.append(
                    pltpu.make_async_remote_copy(
                        src_ref=block.at[span],
                        dst_ref=block.at[span],
                        send_sem=send.at[place],
                        recv_sem=recv.at[place],
                        device_id=peers[name],
                        device_id_type=MESH,
                    )
                )
                place += 1
            self.steps.append(copies)
        self.own = (rows(first + ay * eighth, eighth), rows(second + ax * eighth, eighth))

    def start(self, step):
        for copy in self.steps[step]:
            copy.start()

    def finish(self, step):
        for copy in self.steps[step]:
            copy.wait_recv()

    def drain(self):
        for step in self.steps:
            for copy in step:
                copy.wait_send()


def plus(left, right):
    return (left.astype(F32) + right.astype(F32)).astype(BF)


class Fold:
    def __init__(self, held, from_core, from_one, from_two, send, recv):
        _, _, core, ax, ay, peers = places()
        half = held.shape[0]
        part, quarter, eighth = half // 2, half // 4, half // 8
        self.held = held
        self.from_core = from_core
        self.from_one = from_one
        self.from_two = from_two
        self.quarter, self.eighth = quarter, eighth
        self.give_one = (rows((1 - ax) * quarter, quarter), rows(part + (1 - ay) * quarter, quarter))
        self.keep_one = (rows(ax * quarter, quarter), rows(part + ay * quarter, quarter))
        self.give_two = (
            rows(ax * quarter + (1 - ay) * eighth, eighth),
            rows(part + ay * quarter + (1 - ax) * eighth, eighth),
        )
        self.keep_two = (
            rows(ax * quarter + ay * eighth, eighth),
            rows(part + ay * quarter + ax * eighth, eighth),
        )
        self.inside = (rows((1 - ay) * eighth, eighth), rows((1 - ax) * eighth, eighth))
        self.inside_keep = (rows(ay * eighth, eighth), rows(ax * eighth, eighth))
        self.one = [
            pltpu.make_async_remote_copy(
                src_ref=held.at[self.give_one[p]],
                dst_ref=from_one.at[p],
                send_sem=send.at[p],
                recv_sem=recv.at[p],
                device_id=peers["xy"[p]],
                device_id_type=MESH,
            )
            for p in (0, 1)
        ]
        self.two = [
            pltpu.make_async_remote_copy(
                src_ref=held.at[self.give_two[p]],
                dst_ref=from_two.at[p],
                send_sem=send.at[2 + p],
                recv_sem=recv.at[2 + p],
                device_id=peers["yx"[p]],
                device_id_type=MESH,
            )
            for p in (0, 1)
        ]

    def step_core(self, own):
        for spans in (self.give_one, self.keep_one):
            for p in (0, 1):
                span = spans[p]
                self.held[span] = plus(own[span], self.from_core[span])
            if spans is self.give_one:
                for copy in self.one:
                    copy.start()

    def step_one(self):
        for copy in self.one:
            copy.wait_recv()
        for p in (0, 1):
            self.held[self.give_two[p]] = plus(self.held[self.give_two[p]], self.from_one[p, self.inside[p]])
            self.two[p].start()
        for p in (0, 1):
            self.held[self.keep_two[p]] = plus(self.held[self.keep_two[p]], self.from_one[p, self.inside_keep[p]])

    def step_two(self, result):
        for p in (0, 1):
            self.two[p].wait_recv()
            result[p * self.eighth : (p + 1) * self.eighth] = plus(self.held[self.keep_two[p]], self.from_two[p])

    def drain(self):
        for copy in self.one + self.two:
            copy.wait_send()


class Everyone:
    def __init__(self, total, landing, send, recv, peer_list):
        self.total, self.landing = total, landing
        self.copies = [
            pltpu.make_async_remote_copy(
                src_ref=total.at[step],
                dst_ref=landing.at[step],
                send_sem=send.at[step],
                recv_sem=recv.at[step],
                device_id=peer,
                device_id_type=MESH,
            )
            for step, peer in enumerate(peer_list)
        ]

    def start(self, step):
        self.copies[step].start()

    def finish(self, step):
        self.copies[step].wait_recv()
        self.total[step + 1] = self.total[step] + self.landing[step]

    def drain(self):
        for copy in self.copies:
            copy.wait_send()


DIMS = {"NN": ((1,), (0,)), "NT": ((1,), (1,)), "TN": ((0,), (0,))}
SCALING = 1.0 / math.sqrt(HEAD_DIM)


def dot(left, right, form="NN"):
    return lax.dot_general(left, right, (DIMS[form], ((), ())), preferred_element_type=F32)


def column_sum(values):
    return jnp.sum(values, axis=0, keepdims=True)


def row_mean(values):
    return jnp.mean(values, axis=-1, keepdims=True)


def chunks(count, size, body):
    def run(step, carry):
        body(rows(step * size, size))
        return carry

    lax.fori_loop(0, count // size, run, 0)


def block_body(
    outer,
    x_hbm, cot_hbm, seg_ref, pad_ref, vec_ref, own_a, own_b, own_c,
    out_hbm, grad_in_hbm, summed_out, small_out,
    weights, x_ref, cot, masks, vecs, qkv, ctx, probs, norm_one, scale_one, hidden_low, act, slope,
    acc, d_norm, d_low, d_ctx,
    grads, from_core, from_one, from_two, zone, from_z, outer_in, totals, landing,
    gz_send, gz_recv, g_send, g_recv, v_send, v_recv, local_sem,
    csend, crecv, fsend, frecv, zsend, zrecv, asend, arecv, osend, orecv, ssend, srecv, credit,
):
    dp, z, core, ax, ay, peers = places()
    others = outer_peers(dp, z, outer)
    everyone = [peers[name] for name in ("c", "x", "y", 1, 2)] + others
    tokens, width = x_ref.shape
    side = own_a.shape[0]
    half = side // 2
    eighth = half // 8
    cols = side // 4
    heads = cols // HEAD_DIM
    row_count = tokens // SEQ
    shard_of = {0: z, 1: peers[1]["tensor"], 2: peers[2]["tensor"], 3: peers[3]["tensor"]}
    own_refs = [own_a, own_b, own_c]

    local_copies = [
        pltpu.make_async_copy(x_hbm, x_ref, local_sem.at[0]),
        pltpu.make_async_copy(own_a, weights.at[0, 0], local_sem.at[1]),
        pltpu.make_async_copy(vec_ref, vecs.at[0], local_sem.at[2]),
        pltpu.make_async_copy(own_b, weights.at[1, 0], local_sem.at[3]),
        pltpu.make_async_copy(own_c, weights.at[2, 0], local_sem.at[4]),
        pltpu.make_async_copy(cot_hbm, cot, local_sem.at[5]),
    ]
    for copy in local_copies:
        copy.start()
    greet([peers[name] for name in ("c", "x", "y", 1, 2, 3)] + others)

    spreads, crossing, vec_copies = {}, {}, {}
    gathered = [(k, j) for k in range(3) for j in (1, 2, 3)]
    for k, j in gathered:
        spreads[k, j] = Spread(weights.at[k, j], half, g_send.at[k, j - 1], g_recv.at[k, j - 1])
        crossing[k, j] = [
            pltpu.make_async_remote_copy(
                src_ref=own_refs[k].at[span],
                dst_ref=weights.at[k, j, span],
                send_sem=gz_send.at[k, j - 1, piece],
                recv_sem=gz_recv.at[k, j - 1, piece],
                device_id=peers[j],
                device_id_type=MESH,
            )
            for piece, span in enumerate(spreads[k, j].own)
        ]
    for j in (1, 2, 3):
        vec_copies[j] = pltpu.make_async_remote_copy(
            src_ref=vec_ref,
            dst_ref=vecs.at[j],
            send_sem=v_send.at[j - 1],
            recv_sem=v_recv.at[j - 1],
            device_id=peers[j],
            device_id_type=MESH,
        )
    for k, j in gathered:
        for copy in crossing[k, j]:
            copy.start()
        if k == 0:
            vec_copies[j].start()

    def gather_turn(turn):
        total = len(gathered)
        if turn < total:
            item = gathered[turn]
            for copy in crossing[item]:
                copy.wait_recv()
            spreads[item].start(0)
        for lag in (1, 2):
            if 0 <= turn - lag < total:
                item = gathered[turn - lag]
                spreads[item].finish(lag - 1)
                spreads[item].start(lag)
        if 0 <= turn - 3 < total:
            spreads[gathered[turn - 3]].finish(2)

    def vector(row, slot=0):
        return vecs[slot, row : row + 1, :].astype(F32)

    def build_masks():
        for r in range(row_count):
            place = pl.ds(z * row_count + r, 1)
            seg = jnp.broadcast_to(seg_ref[place, :].astype(F32), (SEQ, SEQ))
            pad = jnp.broadcast_to(pad_ref[place, :], (SEQ, SEQ))
            allowed = (seg == seg.T) & (pad == 1)
            masks[r] = jnp.where(allowed, 0.0, MASKED)

    def project(j):
        bias = vector(0, j)[:, : 3 * cols]
        qkv[j] = (dot(x_ref[...], weights[0, j, : 3 * cols], "NT") + bias).astype(BF)

    def attend(j):
        def one(r, carry):
            span = rows(r * SEQ, SEQ)
            joined = qkv[j, span]
            found = []
            for h in range(heads):
                q, k, v = (joined[:, i * cols + h * HEAD_DIM : i * cols + (h + 1) * HEAD_DIM] for i in range(3))
                scores = dot(q, k, "NT") * SCALING + masks[r]
                weight = jnp.exp(scores - jnp.max(scores, axis=-1, keepdims=True))
                prob = (weight * (1.0 / jnp.sum(weight, axis=-1, keepdims=True))).astype(BF)
                probs[j, r, h] = prob
                found.append(dot(prob, v).astype(BF))
            ctx[j, span] = jnp.concatenate(found, axis=1)
            return carry

        lax.fori_loop(0, row_count, one, 0)

    def project_out():
        total = dot(ctx[0], weights[0, 0, 3 * cols :])
        for j in (1, 2, 3):
            total = total + dot(ctx[j], weights[0, j, 3 * cols :])
        acc[...] = total

    def norm_first():
        b_out, gain, shift = vector(2), vector(3), vector(4)

        def body(span):
            value = acc[span] + b_out + x_ref[span].astype(F32)
            center = value - row_mean(value)
            scale = lax.rsqrt(row_mean(center * center) + EPSILON)
            normal = center * scale
            norm_one[span] = normal
            scale_one[span] = scale
            hidden_low[span] = (normal * gain + shift).astype(BF)

        chunks(tokens, 128, body)

    def feed_in(j):
        bias = vector(1, j)

        def body(span):
            pre = dot(hidden_low[span], weights[1, j]) + bias
            cumulative = 0.5 + 0.5 * lax.erf(pre * (1.0 / math.sqrt(2.0)))
            density = jnp.exp(pre * pre * -0.5) * (1.0 / math.sqrt(2.0 * math.pi))
            act[j, span] = (pre * cumulative).astype(BF)
            slope[j, span] = (cumulative + pre * density).astype(BF)

        chunks(tokens, 128, body)

    def feed_out(j):
        part = dot(act[j], weights[2, j])
        acc[...] = part if j == 0 else acc[...] + part

    def small_add(row, value):
        totals[0, pl.ds(row, 1), : value.shape[1]] += value

    def norm_second():
        gain_a, shift_a, b_outer = vector(3), vector(4), vector(5)
        gain, shift = vector(6), vector(7)

        def body(span):
            value = acc[span] + b_outer + (norm_one[span] * gain_a + shift_a)
            center = value - row_mean(value)
            scale = lax.rsqrt(row_mean(center * center) + EPSILON)
            normal = center * scale
            given = cot[span].astype(F32)
            cot[span] = (normal * gain + shift).astype(BF)
            pulled = given * gain
            grad = scale * (pulled - row_mean(pulled) - normal * row_mean(pulled * normal))
            d_norm[span] = grad
            d_low[span] = grad.astype(BF)
            small_add(3, column_sum(grad))
            small_add(4, column_sum(given * normal))
            small_add(5, column_sum(given))

        chunks(tokens, 128, body)

    def feed_out_back(j):
        def body(span):
            grad = (dot(d_low[span], weights[2, j], "NT") * slope[j, span].astype(F32)).astype(BF)
            act[j, span] = grad
            small_add(12 + shard_of[j], column_sum(grad.astype(F32)))

        chunks(tokens, 256, body)

    def feed_in_back(j, first):
        part = dot(act[j], weights[1, j], "NT")
        acc[...] = part if first else acc[...] + part

    def norm_first_back():
        gain = vector(3)

        def body(span):
            given = acc[span] + d_norm[span]
            normal = norm_one[span]
            pulled = given * gain
            grad = scale_one[span] * (pulled - row_mean(pulled) - normal * row_mean(pulled * normal))
            d_norm[span] = grad
            d_low[span] = grad.astype(BF)
            small_add(0, column_sum(grad))
            small_add(1, column_sum(given * normal))
            small_add(2, column_sum(given))

        chunks(tokens, 128, body)

    def attend_back(j):
        d_ctx[...] = dot(d_low[...], weights[0, j, 3 * cols :], "NT").astype(BF)

        def one(r, carry):
            span = rows(r * SEQ, SEQ)
            joined = qkv[j, span]
            given = d_ctx[span]
            found = [[], [], []]
            for h in range(heads):
                q, k, v = (joined[:, i * cols + h * HEAD_DIM : i * cols + (h + 1) * HEAD_DIM] for i in range(3))
                d_out = given[:, h * HEAD_DIM : (h + 1) * HEAD_DIM]
                prob = probs[j, r, h]
                wide = prob.astype(F32)
                d_prob = dot(d_out, v, "NT")
                inner = jnp.sum(d_prob * wide, axis=-1, keepdims=True)
                d_score = (wide * (d_prob - inner)).astype(BF)
                found[0].append((dot(d_score, k) * SCALING).astype(BF))
                found[1].append((dot(d_score, q, "TN") * SCALING).astype(BF))
                found[2].append(dot(prob, d_out, "TN").astype(BF))
            joined_grad = jnp.concatenate(found[0] + found[1] + found[2], axis=1)
            qkv[j, span] = joined_grad
            small_add(8 + shard_of[j], column_sum(joined_grad.astype(F32)))
            return carry

        lax.fori_loop(0, row_count, one, 0)

    def input_back(j):
        d_norm[...] = d_norm[...] + dot(qkv[j], weights[0, j, : 3 * cols])

    mine, theirs = rows(core * half, half), rows((1 - core) * half, half)
    mine_cols = pl.ds(pl.multiple_of(core * half, 128), half)
    their_cols = pl.ds(pl.multiple_of((1 - core) * half, 128), half)
    order = [(k, j) for k in range(3) for j in (1, 2, 3, 0)]
    swaps = {
        (k, j): pltpu.make_async_remote_copy(
            src_ref=grads.at[k % 2, j, theirs],
            dst_ref=from_core.at[k % 2, j],
            send_sem=csend.at[k, j],
            recv_sem=crecv.at[k, j],
            device_id=peers["c"],
            device_id_type=MESH,
        )
        for k, j in order
    }
    folds = {
        (k, j): Fold(
            grads.at[k % 2, j, mine], from_core.at[k % 2, j], from_one.at[k, j], from_two.at[k, j],
            fsend.at[k, j], frecv.at[k, j],
        )
        for k, j in order
    }
    over = {
        (k, j): pltpu.make_async_remote_copy(
            src_ref=zone.at[k, j],
            dst_ref=from_z.at[k, j - 1],
            send_sem=zsend.at[k, j - 1],
            recv_sem=zrecv.at[k, j - 1],
            device_id=peers[j],
            device_id_type=MESH,
        )
        for k, j in order
        if j
    }
    sums = [Spread(summed_out.at[k], half, asend.at[k], arecv.at[k]) for k in range(3)]
    tiny = Everyone(totals, landing, ssend, srecv, everyone)

    def settle(k):
        for j in (1, 2, 3):
            over[k, j].wait_recv()
        summed = zone[k, 0].astype(F32)
        for j in (1, 2, 3):
            summed = summed + from_z[k, j - 1].astype(F32)
        for step, peer in enumerate(others):
            outer_in[k, step, 0] = summed.astype(BF)
            copy = pltpu.make_async_remote_copy(
                src_ref=outer_in.at[k, step, 0],
                dst_ref=outer_in.at[k, step, 1],
                send_sem=osend.at[k, step],
                recv_sem=orecv.at[k, step],
                device_id=peer,
                device_id_type=MESH,
            )
            copy.start()
            copy.wait()
            summed = outer_in[k, step, 0].astype(F32) + outer_in[k, step, 1].astype(F32)
        for p in (0, 1):
            summed_out[k, sums[k].own[p]] = summed[p * eighth : (p + 1) * eighth].astype(BF)
        sums[k].start(0)

    def drain(item):
        swaps[item].wait_send()
        folds[item].drain()

    def grad_block(k, j):
        if k == 0:
            for span, picked in ((theirs, their_cols), (mine, mine_cols)):
                grads[0, j, span] = dot(act[j, :, picked], d_low[...], "TN").astype(BF)
                if span is theirs:
                    swaps[k, j].start()
        elif k == 1:
            for span, picked in ((theirs, their_cols), (mine, mine_cols)):
                grads[1, j, span] = dot(hidden_low[:, picked], act[j], "TN").astype(BF)
                if span is theirs:
                    swaps[k, j].start()
        else:
            drain((0, j))
            pl.semaphore_wait(credit.at[j], 1)
            grads[0, j, : 3 * cols] = dot(qkv[j], x_ref[...], "TN").astype(BF)
            grads[0, j, 3 * cols :] = dot(ctx[j], d_low[...], "TN").astype(BF)
            swaps[k, j].start()

    def reduce_turn(turn):
        total = len(order)
        if turn < total:
            item = order[turn]
            swaps[item].wait_recv()
            folds[item].step_core(grads.at[item[0] % 2, item[1], mine])
            if item[0] == 0:
                pl.semaphore_signal(credit.at[item[1]], inc=1, device_id=peers["c"], device_id_type=MESH)
        if 0 <= turn - 1 < total:
            folds[order[turn - 1]].step_one()
        if 0 <= turn - 2 < total:
            item = order[turn - 2]
            folds[item].step_two(zone.at[item[0], item[1]])
            if item[1]:
                over[item].start()
        if turn - 3 >= 0 and (turn - 3) % 4 == 3 and turn - 3 < total:
            settle((turn - 3) // 4)
        for step in (0, 1, 2):
            back = turn - 4 - step
            if back >= 0 and back % 4 == 3 and back < total:
                k = back // 4
                sums[k].finish(step)
                if step < 2:
                    sums[k].start(step + 1)

    local_copies[0].wait()
    local_copies[1].wait()
    local_copies[2].wait()
    build_masks()
    totals[0] = jnp.zeros_like(totals[0])
    project(0)
    gather_turn(0)
    attend(0)
    gather_turn(1)
    gather_turn(2)
    for j in (1, 2, 3):
        gather_turn(2 + j)
        if j == 1:
            for i in (1, 2, 3):
                vec_copies[i].wait_recv()
        project(j)
        attend(j)
    project_out()
    norm_first()
    local_copies[3].wait()
    feed_in(0)
    for j in (1, 2, 3):
        gather_turn(5 + j)
        feed_in(j)
    local_copies[4].wait()
    feed_out(0)
    for j in (1, 2, 3):
        gather_turn(8 + j)
        feed_out(j)
    local_copies[5].wait()
    norm_second()
    out_copy = pltpu.make_async_copy(cot, out_hbm, local_sem.at[0])
    out_copy.start()

    for turn, (k, j) in enumerate(order):
        if k == 2:
            if j == 1:
                norm_first_back()
            attend_back(j)
        grad_block(k, j)
        if k == 0:
            feed_out_back(j)
        elif k == 1:
            feed_in_back(j, j == 1)
        else:
            input_back(j)
        reduce_turn(turn)
    grad_in_copy = pltpu.make_async_copy(d_norm, grad_in_hbm, local_sem.at[1])
    grad_in_copy.start()
    tiny.start(0)
    for extra in range(6):
        if extra < len(everyone):
            tiny.finish(extra)
            if extra + 1 < len(everyone):
                tiny.start(extra + 1)
        reduce_turn(len(order) + extra)
    for extra in range(6, len(everyone)):
        tiny.finish(extra)
        if extra + 1 < len(everyone):
            tiny.start(extra + 1)
    small_out[...] = totals[len(everyone)]

    for item in gathered:
        for copy in crossing[item]:
            copy.wait_send()
        spreads[item].drain()
    for j in (1, 2, 3):
        vec_copies[j].wait_send()
    for item in order:
        if item[0]:
            drain(item)
        if item[1]:
            over[item].wait_send()
    for spread in sums:
        spread.drain()
    tiny.drain()
    out_copy.wait()
    grad_in_copy.wait()


def block(outer, x, cot, seg, pad, vec, own_a, own_b, own_c):
    tokens, width = x.shape
    side = own_a.shape[0]
    half, cols = side // 2, side // 4
    heads = cols // HEAD_DIM
    row_count = tokens // SEQ
    steps = 5 + int(math.log2(outer))
    more = max(steps - 5, 1)
    outer_rows = half // 4 if outer > 1 else 16
    dma = pltpu.SemaphoreType.DMA
    vmem = pltpu.VMEM
    any_space = pl.BlockSpec(memory_space=pl.ANY)
    in_vmem = pl.BlockSpec(memory_space=pltpu.VMEM)
    return pl.pallas_call(
        functools.partial(block_body, outer),
        out_shape=(
            jax.ShapeDtypeStruct((tokens, width), BF),
            jax.ShapeDtypeStruct((tokens, width), F32),
            jax.ShapeDtypeStruct((3, side, width), BF),
            jax.ShapeDtypeStruct((16, width), F32),
        ),
        in_specs=[any_space, any_space, in_vmem, in_vmem, any_space, any_space, any_space, any_space],
        out_specs=(any_space, any_space, in_vmem, in_vmem),
        scratch_shapes=[
            vmem((3, 4, side, width), BF),
            vmem((tokens, width), BF),
            vmem((tokens, width), BF),
            vmem((row_count, SEQ, SEQ), F32),
            vmem((4, 16, width), BF),
            vmem((4, tokens, 3 * cols), BF),
            vmem((4, tokens, cols), BF),
            vmem((4, row_count, heads, SEQ, SEQ), BF),
            vmem((tokens, width), F32),
            vmem((tokens, 1), F32),
            vmem((tokens, width), BF),
            vmem((4, tokens, side), BF),
            vmem((4, tokens, side), BF),
            vmem((tokens, width), F32),
            vmem((tokens, width), F32),
            vmem((tokens, width), BF),
            vmem((tokens, cols), BF),
            vmem((2, 4, side, width), BF),
            vmem((2, 4, half, width), BF),
            vmem((3, 4, 2, half // 4, width), BF),
            vmem((3, 4, 2, half // 8, width), BF),
            vmem((3, 4, half // 4, width), BF),
            vmem((3, 3, half // 4, width), BF),
            vmem((3, more, 2, outer_rows, width), BF),
            vmem((steps + 1, 16, width), F32),
            vmem((steps, 16, width), F32),
            dma((3, 3, 2)), dma((3, 3, 2)), dma((3, 3, 5)), dma((3, 3, 5)), dma((3,)), dma((3,)), dma((6,)),
            dma((3, 4)), dma((3, 4)), dma((3, 4, 4)), dma((3, 4, 4)), dma((3, 3)), dma((3, 3)),
            dma((3, 5)), dma((3, 5)), dma((3, more)), dma((3, more)), dma((steps,)), dma((steps,)),
            pltpu.SemaphoreType.REGULAR((4,)),
        ],
        compiler_params=pltpu.CompilerParams(
            collective_id=0, has_side_effects=True, vmem_limit_bytes=67043328
        ),
        name="block",
    )(x, cot, seg, pad, vec, own_a, own_b, own_c)


def local(
    outer, block_input, cotangent, segment_ids, pad_mask,
    w_query, b_query, w_key, w_value, b_value, w_out, b_out, gain_one, shift_one,
    w_inner, b_inner, w_outer, b_outer, gain_two, shift_two,
):
    tokens, width = block_input.shape
    cols = w_query.shape[1]
    z = lax.axis_index("tensor")
    own_a = jnp.concatenate([w_query.T, w_key.T, w_value.T, w_out], axis=0)
    zero = jnp.zeros((cols,), BF)
    vec = jnp.pad(
        jnp.stack(
            [
                jnp.concatenate([b_query, zero, b_value, zero]), b_inner,
                b_out, gain_one, shift_one, b_outer, gain_two, shift_two,
            ]
        ),
        ((0, 8), (0, 0)),
    )
    output, grad_input, summed, small = block(
        outer, block_input, cotangent, segment_ids.reshape(-1, SEQ), pad_mask.reshape(-1, SEQ),
        vec, own_a, w_inner, w_outer,
    )
    summed = summed.astype(F32)
    own = lax.dynamic_slice(small, (8 + z, 0), (1, width))[0]
    own_inner = lax.dynamic_slice(small, (12 + z, 0), (1, width))[0]
    return (
        output,
        grad_input,
        summed[2, :cols].T,
        own[:cols],
        summed[2, cols : 2 * cols].T,
        summed[2, 2 * cols : 3 * cols].T,
        own[2 * cols : 3 * cols],
        summed[2, 3 * cols :],
        small[0],
        small[1],
        small[2],
        summed[1],
        own_inner,
        summed[0],
        small[3],
        small[4],
        small[5],
    )


def solution(mesh):
    outer = mesh.shape["dp"] // GROUP
    row, col, both, rep = P("tensor", None), P(None, "tensor"), P(("dp", "tensor"), None), P()
    part = P("tensor")
    return jax.shard_map(
        functools.partial(local, outer),
        mesh=mesh,
        in_specs=(
            both, both, P("dp"), P("dp"), col, part, col, col, part, row, rep, rep, rep,
            col, part, row, rep, rep, rep,
        ),
        out_specs=(
            both, both, col, part, col, col, part, row, rep, rep, rep, col, part, row, rep, rep, rep,
        ),
        check_vma=False,
    )
```

profile of v0, /device:TPU:1, one launch (start us, length us, event | category | flops | bytes accessed | tf_op | source)
XLA Modules:
  0.0 198.4 jit_solution(5089391149531246971)
XLA Ops:
  0.7 0.8 pad_maximum_fusion.1
  1.4 0.7 stack.29
  2.1 0.7 stack.30
  2.8 0.7 stack.31
  3.5 0.7 stack.28
  4.2 0.7 stack.32
  4.9 0.7 stack.33
  5.5 0.7 stack.34
  6.3 0.6 pad.4.vec_ref
  6.9 2.3 %pad_maximum_fusion.own_a = bf16[768,768]{1,0:T(8,128)(2,1)} fusion(bf16[192,768]{1,0:T(8,128)(2,1)} %param.28, bf16[192,768]{1,0:T(8,128)(2,1)} %bitcast.25, bf16[192,768]{1,0:T(8,128)(2,1)} %bitcast.26, bf16[192,768]{1,0:T(8,128)(2,1)} %bitcast.27), kind=kLoop, calls=%fused_computation.2 | loop fusion | flops 4718592 | bytes 2359296 | tf_op jit(solution)/shard_map/concatenate | solution.py:720
  9.2 176.8 %block.1 = (bf16[512,768]{1,0:T(8,128)(2,1)}, f32[512,768]{1,0:T(8,128)}, bf16[3,768,768]{2,1,0:T(8,128)(2,1)}, f32[16,768]{1,0:T(8,128)}) custom-call(bf16[512,768]{1,0:T(8,128)(2,1)} %x_hbm.1, bf16[512,768]{1,0:T(8,128)(2,1)} %cot_hbm.1, s32[16,128]{1,0:T(8,128)} %bitcast.28, s32[16,128]{1,0:T(8,128)} %bitcast.29, bf16[16,768]{1,0:T(8,128)(2,1)} %pad.4.vec_ref, ...), custom_call_target="tpu_custom_call" | custom-call | tf_op jit(solution)/shard_map/block/pallas_call | solution.py:663
  186.0 1.4 fusion
  187.4 1.6 slice_reduce_fusion
  189.0 2.6 %convert_element_type.5 = f32[3,768,768]{2,1,0:T(8,128)S(1)} convert(bf16[3,768,768]{2,1,0:T(8,128)(2,1)} %get-tuple-element.23) | non-fusion elementwise | flops 1769472 | bytes 10616832 | tf_op jit(solution)/shard_map/convert_element_type | solution.py:735
  191.6 1.4 slice_bitcast_fusion.2
  193.1 0.0 copy-start.1
  193.1 2.5 %slice_bitcast_fusion = (f32[768,768]{1,0:T(8,128)}, f32[768,768]{1,0:T(8,128)}) fusion(f32[3,768,768]{2,1,0:T(8,128)S(1)} %convert_element_type.5), kind=kLoop, calls=%fused_computation | loop fusion | bytes 9437184 | tf_op jit(solution)/shard_map/squeeze | solution.py:752
  195.6 0.0 copy-start
  195.6 0.0 copy-done.1
  195.6 0.9 copy.38
  196.4 0.8 copy-done
  197.2 1.1 copy.39
  (3 shorter events, 0.1 us)
Async XLA Ops:
  193.1 2.5 %copy-start.1 = (bf16[512,768]{1,0:T(8,128)(2,1)S(1)}, bf16[512,768]{1,0:T(8,128)(2,1)}, u32[]{:S(2)}) copy-start(bf16[512,768]{1,0:T(8,128)(2,1)} %get-tuple-element.57) | copy-start | bytes 2359300
  195.6 1.7 copy-start
where the time goes:
time: 199 us; the launch traced here: 198 us
  Pallas kernels  177 us (89%)
  local copies, waits for them, and re-layouts  15.2 us (8%)
  other arithmetic  5.66 us (3%)
    pallas_call x1, Pallas kernels, block(): pl.pallas_call(functools.partial(block_body, outer), out_shape=(jax.Shape...  177 us
    another operation x9, local copies, waits for them, and re-layouts, local(): jnp.stack([jnp.concatenate([b_query, zero, b_value, zero]), b_inner, b_ou...  4.85 us

commit v1 on v0

--- a/solution.py
+++ b/solution.py
@@ -16,6 +16,7 @@
 F32 = jnp.float32
 MESH = pl.DeviceIdType.MESH
 GROUP = 8
+WIDE = (2,)
 
 
 def places():
@@ -35,6 +36,13 @@
     return dp, z, core, along_x, along_y, peers
 
 
+def line_order(z):
+    low, high = z % 2, z // 2
+    middle = low + high - 2 * low * high
+    shards = (z, z + 1 - 2 * low, (1 - middle) * ((z + 2) % 4) + middle * (3 - z), middle * ((z + 2) % 4) + (1 - middle) * (3 - z))
+    return middle, shards, (0, 1, 3 - middle, 3 - middle)
+
+
 def outer_peers(dp, z, outer):
     found = []
     weight = GROUP
@@ -45,19 +53,12 @@
     return found
 
 
-def greet(peer_list):
-    barrier = pltpu.get_barrier_semaphore()
-    for peer in peer_list:
-        pl.semaphore_signal(barrier, inc=1, device_id=peer, device_id_type=MESH)
-    pl.semaphore_wait(barrier, len(peer_list))
-
-
 def rows(start, size):
     return pl.ds(pl.multiple_of(start, 16), size)
 
 
 class Spread:
-    def __init__(self, block, half, send, recv):
+    def __init__(self, block, half, send, recv, wide=False):
         _, _, core, ax, ay, peers = places()
         base = core * half
         part = half // 2
@@ -72,9 +73,9 @@
             ((rows(base, half), "c"),),
         )
         place = 0
-        for step in plan:
+        for number, step in enumerate(plan):
             copies = []
-            for span, name in step:
+            for span, name in () if wide and number == 0 else step:
                 copies.append(
                     pltpu.make_async_remote_copy(
                         src_ref=block.at[span],
@@ -88,6 +89,8 @@
                 place += 1
             self.steps.append(copies)
         self.own = (rows(first + ay * eighth, eighth), rows(second + ax * eighth, eighth))
+        if wide:
+            self.own = (rows(first, quarter), rows(second, quarter))
 
     def start(self, step):
         for copy in self.steps[step]:
@@ -233,86 +236,136 @@
 
 def block_body(
     outer,
-    x_hbm, cot_hbm, seg_ref, pad_ref, vec_ref, own_a, own_b, own_c,
-    out_hbm, grad_in_hbm, summed_out, small_out,
-    weights, x_ref, cot, masks, vecs, qkv, ctx, probs, norm_one, scale_one, hidden_low, act, slope,
+    x_hbm, cot_hbm, seg_ref, pad_ref, w_query, w_key, w_value, w_out, own_b, own_c,
+    b_query, b_value, b_inner, b_out, gain_one, shift_one, b_outer, gain_two, shift_two,
+    out_hbm, grad_in_hbm, summed_hbm, small_hbm,
+    weights, x_ref, cot, masks, vecs, qkv, ctx, probs, norm_one, scale_one, hidden_low, act, shared,
     acc, d_norm, d_low, d_ctx,
     grads, from_core, from_one, from_two, zone, from_z, outer_in, totals, landing,
-    gz_send, gz_recv, g_send, g_recv, v_send, v_recv, local_sem,
+    gz_send, gz_recv, g_send, g_recv, v_send, v_recv, local_sem, early_sem,
     csend, crecv, fsend, frecv, zsend, zrecv, asend, arecv, osend, orecv, ssend, srecv, credit,
 ):
     dp, z, core, ax, ay, peers = places()
     others = outer_peers(dp, z, outer)
     everyone = [peers[name] for name in ("c", "x", "y", 1, 2)] + others
     tokens, width = x_ref.shape
-    side = own_a.shape[0]
+    side = own_b.shape[0]
     half = side // 2
     eighth = half // 8
     cols = side // 4
     heads = cols // HEAD_DIM
     row_count = tokens // SEQ
-    shard_of = {0: z, 1: peers[1]["tensor"], 2: peers[2]["tensor"], 3: peers[3]["tensor"]}
-    own_refs = [own_a, own_b, own_c]
+    slope = [shared.at[u * tokens : (u + 1) * tokens] for u in range(4)]
+    summed_out = [shared.at[k * side : (k + 1) * side] for k in range(3)]
+    middle, shard_of, landing_place = line_order(z)
+    line = {u: {"dp": dp, "tensor": shard_of[u]} for u in (1, 2, 3)}
 
     local_copies = [
         pltpu.make_async_copy(x_hbm, x_ref, local_sem.at[0]),
-        pltpu.make_async_copy(own_a, weights.at[0, 0], local_sem.at[1]),
-        pltpu.make_async_copy(vec_ref, vecs.at[0], local_sem.at[2]),
-        pltpu.make_async_copy(own_b, weights.at[1, 0], local_sem.at[3]),
-        pltpu.make_async_copy(own_c, weights.at[2, 0], local_sem.at[4]),
-        pltpu.make_async_copy(cot_hbm, cot, local_sem.at[5]),
+        pltpu.make_async_copy(w_out, weights.at[0, 0, 3 * cols :], local_sem.at[1]),
+        pltpu.make_async_copy(own_b, weights.at[1, 0], local_sem.at[2]),
+        pltpu.make_async_copy(own_c, weights.at[2, 0], local_sem.at[3]),
+        pltpu.make_async_copy(cot_hbm, cot, local_sem.at[4]),
+    ] + [
+        pltpu.make_async_copy(ref, weights.at[0, 0, part * cols : (part + 1) * cols], local_sem.at[5 + part])
+        for part, ref in enumerate((w_query, w_key, w_value))
     ]
-    for copy in local_copies:
-        copy.start()
-    greet([peers[name] for name in ("c", "x", "y", 1, 2, 3)] + others)
-
-    spreads, crossing, vec_copies = {}, {}, {}
-    gathered = [(k, j) for k in range(3) for j in (1, 2, 3)]
-    for k, j in gathered:
-        spreads[k, j] = Spread(weights.at[k, j], half, g_send.at[k, j - 1], g_recv.at[k, j - 1])
-        crossing[k, j] = [
-            pltpu.make_async_remote_copy(
-                src_ref=own_refs[k].at[span],
-                dst_ref=weights.at[k, j, span],
-                send_sem=gz_send.at[k, j - 1, piece],
-                recv_sem=gz_recv.at[k, j - 1, piece],
-                device_id=peers[j],
-                device_id_type=MESH,
+    for number in (5, 6, 7, 1, 0, 2, 3, 4):
+        local_copies[number].start()
+    barrier = pltpu.get_barrier_semaphore()
+    greeted = [peers[name] for name in ("c", "x", "y", 1, 2, 3)] + others
+    for peer in greeted:
+        pl.semaphore_signal(barrier, inc=1, device_id=peer, device_id_type=MESH)
+
+    spreads, arrivals, vec_copies = {}, {}, {}
+    gathered = [(k, u) for k in range(3) for u in (1, 2, 3)]
+
+    def hop(k, source, target, peer):
+        found = []
+        for piece, span in enumerate(spreads[k, target].own):
+            src = weights.at[k, source, span]
+            if source == 0 and k:
+                src = (None, own_b, own_c)[k].at[span]
+            found.append(
+                pltpu.make_async_remote_copy(
+                    src_ref=src,
+                    dst_ref=weights.at[k, target, span],
+                    send_sem=gz_send.at[k, target - 1, 0 if peer is peers[1] else 1, piece],
+                    recv_sem=gz_recv.at[k, target - 1, piece],
+                    device_id=peer,
+                    device_id_type=MESH,
+                )
             )
-            for piece, span in enumerate(spreads[k, j].own)
-        ]
-    for j in (1, 2, 3):
-        vec_copies[j] = pltpu.make_async_remote_copy(
-            src_ref=vec_ref,
-            dst_ref=vecs.at[j],
-            send_sem=v_send.at[j - 1],
-            recv_sem=v_recv.at[j - 1],
-            device_id=peers[j],
+        return found
+
+    for k, u in gathered:
+        spreads[k, u] = Spread(weights.at[k, u], half, g_send.at[k, u - 1], g_recv.at[k, u - 1], k in WIDE)
+    near = {k: hop(k, 0, 1, peers[1]) for k in range(3)}
+    across = {(k, 2): hop(k, 0, 2, peers[3]) for k in range(3)}
+    across.update({(k, 3): hop(k, 1, 3, peers[3]) for k in range(3)})
+    onward = {(k, u): hop(k, u, u, peers[1]) for k in range(3) for u in (2, 3)}
+    for u in (1, 2, 3):
+        vec_copies[u] = pltpu.make_async_remote_copy(
+            src_ref=vecs.at[0],
+            dst_ref=vecs.at[landing_place[u]],
+            send_sem=v_send.at[u - 1],
+            recv_sem=v_recv.at[landing_place[u] - 1],
+            device_id=line[u],
             device_id_type=MESH,
         )
-    for k, j in gathered:
-        for copy in crossing[k, j]:
+
+    def begin(copies):
+        for copy in copies:
             copy.start()
-        if k == 0:
-            vec_copies[j].start()
+
+    def send_own(k):
+        begin(near[k])
+        pl.when(middle == 1)(lambda: begin(across[k, 2]))
+
+    def line_turn(turn):
+        if turn >= len(gathered):
+            return
+        k, u = gathered[turn]
+        for copy in {1: near[k], 2: across[k, 2], 3: across[k, 3]}[u]:
+            copy.wait_recv()
+
+        def further():
+            if u == 1:
+                begin(across[k, 3])
+            else:
+                begin(onward[k, u])
+
+        pl.when(middle == 1)(further)
+        if u == 2 and k < 2:
+            send_own(k + 1)
 
     def gather_turn(turn):
         total = len(gathered)
+        if turn == 0:
+            line_turn(0)
+        if turn == 1:
+            line_turn(1)
         if turn < total:
-            item = gathered[turn]
-            for copy in crossing[item]:
-                copy.wait_recv()
-            spreads[item].start(0)
+            spreads[gathered[turn]].start(1 if gathered[turn][0] in WIDE else 0)
         for lag in (1, 2):
             if 0 <= turn - lag < total:
                 item = gathered[turn - lag]
-                spreads[item].finish(lag - 1)
-                spreads[item].start(lag)
-        if 0 <= turn - 3 < total:
-            spreads[gathered[turn - 3]].finish(2)
+                if lag == 1 and item[0] in WIDE:
+                    spreads[item].finish(1)
+                    spreads[item].start(2)
+                elif item[0] not in WIDE:
+                    spreads[item].finish(lag - 1)
+                    spreads[item].start(lag)
+        line_turn(turn + 1 if turn else 9)
+        back = turn - 3
+        if 0 <= back < total and gathered[back][0] not in WIDE:
+            spreads[gathered[back]].finish(2)
+        back = turn - 2
+        if 0 <= back < total and gathered[back][0] in WIDE:
+            spreads[gathered[back]].finish(2)
 
     def vector(row, slot=0):
-        return vecs[slot, row : row + 1, :].astype(F32)
+        return vecs[slot, row : row + 1, :]
 
     def build_masks():
         for r in range(row_count):
@@ -324,24 +377,35 @@
 
     def project(j):
         bias = vector(0, j)[:, : 3 * cols]
-        qkv[j] = (dot(x_ref[...], weights[0, j, : 3 * cols], "NT") + bias).astype(BF)
+
+        def body(span):
+            qkv[j, span] = (dot(x_ref[span], weights[0, j, : 3 * cols], "NT") + bias).astype(BF)
+
+        chunks(tokens, 256, body)
+
+    def head(joined, part, h):
+        return joined[:, part * cols + h * HEAD_DIM : part * cols + (h + 1) * HEAD_DIM]
+
+    units = [(r, h) for r in range(row_count) for h in range(heads)]
+
+    def spans(r):
+        return slice(r * SEQ, (r + 1) * SEQ)
 
     def attend(j):
-        def one(r, carry):
-            span = rows(r * SEQ, SEQ)
-            joined = qkv[j, span]
-            found = []
-            for h in range(heads):
-                q, k, v = (joined[:, i * cols + h * HEAD_DIM : i * cols + (h + 1) * HEAD_DIM] for i in range(3))
-                scores = dot(q, k, "NT") * SCALING + masks[r]
-                weight = jnp.exp(scores - jnp.max(scores, axis=-1, keepdims=True))
-                prob = (weight * (1.0 / jnp.sum(weight, axis=-1, keepdims=True))).astype(BF)
-                probs[j, r, h] = prob
-                found.append(dot(prob, v).astype(BF))
-            ctx[j, span] = jnp.concatenate(found, axis=1)
-            return carry
-
-        lax.fori_loop(0, row_count, one, 0)
+        joined = [qkv[j, spans(r)] for r in range(row_count)]
+        scores = [
+            dot(head(joined[r], 0, h), head(joined[r], 1, h), "NT") * SCALING + masks[r] for r, h in units
+        ]
+        found = []
+        for (r, h), score in zip(units, scores):
+            weight = jnp.exp(score - jnp.max(score, axis=-1, keepdims=True))
+            found.append((weight * (1.0 / jnp.sum(weight, axis=-1, keepdims=True))).astype(BF))
+        mixed = []
+        for (r, h), prob in zip(units, found):
+            probs[j, r, h] = prob
+            mixed.append(dot(prob, head(joined[r], 2, h)).astype(BF))
+        for r in range(row_count):
+            ctx[j, spans(r)] = jnp.concatenate(mixed[r * heads : (r + 1) * heads], axis=1)
 
     def project_out():
         total = dot(ctx[0], weights[0, 0, 3 * cols :])
@@ -371,7 +435,7 @@
             cumulative = 0.5 + 0.5 * lax.erf(pre * (1.0 / math.sqrt(2.0)))
             density = jnp.exp(pre * pre * -0.5) * (1.0 / math.sqrt(2.0 * math.pi))
             act[j, span] = (pre * cumulative).astype(BF)
-            slope[j, span] = (cumulative + pre * density).astype(BF)
+            slope[j][span] = (cumulative + pre * density).astype(BF)
 
         chunks(tokens, 128, body)
 
@@ -405,15 +469,18 @@
 
     def feed_out_back(j):
         def body(span):
-            grad = (dot(d_low[span], weights[2, j], "NT") * slope[j, span].astype(F32)).astype(BF)
+            grad = (dot(d_low[span], weights[2, j], "NT") * slope[j][span].astype(F32)).astype(BF)
             act[j, span] = grad
             small_add(12 + shard_of[j], column_sum(grad.astype(F32)))
 
         chunks(tokens, 256, body)
 
     def feed_in_back(j, first):
-        part = dot(act[j], weights[1, j], "NT")
-        acc[...] = part if first else acc[...] + part
+        def body(span):
+            part = dot(act[j, span], weights[1, j], "NT")
+            acc[span] = part if first else acc[span] + part
+
+        chunks(tokens, 256, body)
 
     def norm_first_back():
         gain = vector(3)
@@ -433,32 +500,32 @@
 
     def attend_back(j):
         d_ctx[...] = dot(d_low[...], weights[0, j, 3 * cols :], "NT").astype(BF)
-
-        def one(r, carry):
-            span = rows(r * SEQ, SEQ)
-            joined = qkv[j, span]
-            given = d_ctx[span]
-            found = [[], [], []]
-            for h in range(heads):
-                q, k, v = (joined[:, i * cols + h * HEAD_DIM : i * cols + (h + 1) * HEAD_DIM] for i in range(3))
-                d_out = given[:, h * HEAD_DIM : (h + 1) * HEAD_DIM]
-                prob = probs[j, r, h]
-                wide = prob.astype(F32)
-                d_prob = dot(d_out, v, "NT")
-                inner = jnp.sum(d_prob * wide, axis=-1, keepdims=True)
-                d_score = (wide * (d_prob - inner)).astype(BF)
-                found[0].append((dot(d_score, k) * SCALING).astype(BF))
-                found[1].append((dot(d_score, q, "TN") * SCALING).astype(BF))
-                found[2].append(dot(prob, d_out, "TN").astype(BF))
-            joined_grad = jnp.concatenate(found[0] + found[1] + found[2], axis=1)
-            qkv[j, span] = joined_grad
-            small_add(8 + shard_of[j], column_sum(joined_grad.astype(F32)))
-            return carry
-
-        lax.fori_loop(0, row_count, one, 0)
+        joined = [qkv[j, spans(r)] for r in range(row_count)]
+        given = [d_ctx[spans(r)] for r in range(row_count)]
+        d_outs = [given[r][:, h * HEAD_DIM : (h + 1) * HEAD_DIM] for r, h in units]
+        d_probs = [dot(d_out, head(joined[r], 2, h), "NT") for (r, h), d_out in zip(units, d_outs)]
+        prob_list = [probs[j, r, h] for r, h in units]
+        d_scores = []
+        for d_prob, prob in zip(d_probs, prob_list):
+            wide = prob.astype(F32)
+            inner = jnp.sum(d_prob * wide, axis=-1, keepdims=True)
+            d_scores.append((wide * (d_prob - inner)).astype(BF))
+        d_values = [dot(prob, d_out, "TN").astype(BF) for prob, d_out in zip(prob_list, d_outs)]
+        d_queries = [(dot(ds, head(joined[r], 1, h)) * SCALING).astype(BF) for (r, h), ds in zip(units, d_scores)]
+        d_keys = [(dot(ds, head(joined[r], 0, h), "TN") * SCALING).astype(BF) for (r, h), ds in zip(units, d_scores)]
+        total = jnp.zeros((1, 3 * cols), F32)
+        for r in range(row_count):
+            mine_heads = slice(r * heads, (r + 1) * heads)
+            joined_grad = jnp.concatenate(d_queries[mine_heads] + d_keys[mine_heads] + d_values[mine_heads], axis=1)
+            qkv[j, spans(r)] = joined_grad
+            total = total + column_sum(joined_grad.astype(F32))
+        small_add(8 + shard_of[j], total)
 
     def input_back(j):
-        d_norm[...] = d_norm[...] + dot(qkv[j], weights[0, j, : 3 * cols])
+        def body(span):
+            d_norm[span] = d_norm[span] + dot(qkv[j, span], weights[0, j, : 3 * cols])
+
+        chunks(tokens, 256, body)
 
     mine, theirs = rows(core * half, half), rows((1 - core) * half, half)
     mine_cols = pl.ds(pl.multiple_of(core * half, 128), half)
@@ -485,21 +552,28 @@
     over = {
         (k, j): pltpu.make_async_remote_copy(
             src_ref=zone.at[k, j],
-            dst_ref=from_z.at[k, j - 1],
+            dst_ref=from_z.at[k, landing_place[j] - 1],
             send_sem=zsend.at[k, j - 1],
-            recv_sem=zrecv.at[k, j - 1],
-            device_id=peers[j],
+            recv_sem=zrecv.at[k, landing_place[j] - 1],
+            device_id=line[j],
             device_id_type=MESH,
         )
         for k, j in order
         if j
     }
-    sums = [Spread(summed_out.at[k], half, asend.at[k], arecv.at[k]) for k in range(3)]
+    sums = [Spread(summed_out[k], half, asend.at[k], arecv.at[k]) for k in range(3)]
     tiny = Everyone(totals, landing, ssend, srecv, everyone)
 
     def settle(k):
-        for j in (1, 2, 3):
-            over[k, j].wait_recv()
+        for place in range(3):
+            pltpu.make_async_remote_copy(
+                src_ref=zone.at[k, 1],
+                dst_ref=from_z.at[k, place],
+                send_sem=zsend.at[k, place],
+                recv_sem=zrecv.at[k, place],
+                device_id=peers[1],
+                device_id_type=MESH,
+            ).wait_recv()
         summed = zone[k, 0].astype(F32)
         for j in (1, 2, 3):
             summed = summed + from_z[k, j - 1].astype(F32)
@@ -517,7 +591,7 @@
             copy.wait()
             summed = outer_in[k, step, 0].astype(F32) + outer_in[k, step, 1].astype(F32)
         for p in (0, 1):
-            summed_out[k, sums[k].own[p]] = summed[p * eighth : (p + 1) * eighth].astype(BF)
+            summed_out[k][sums[k].own[p]] = summed[p * eighth : (p + 1) * eighth].astype(BF)
         sums[k].start(0)
 
     def drain(item):
@@ -528,8 +602,11 @@
         if k == 0:
             for span, picked in ((theirs, their_cols), (mine, mine_cols)):
                 grads[0, j, span] = dot(act[j, :, picked], d_low[...], "TN").astype(BF)
-                if span is theirs:
+                if span is theirs and j:
                     swaps[k, j].start()
+            feed_out_back(j)
+            if j == 0:
+                swaps[k, j].start()
         elif k == 1:
             for span, picked in ((theirs, their_cols), (mine, mine_cols)):
                 grads[1, j, span] = dot(hidden_low[:, picked], act[j], "TN").astype(BF)
@@ -566,12 +643,29 @@
                 sums[k].finish(step)
                 if step < 2:
                     sums[k].start(step + 1)
-
-    local_copies[0].wait()
-    local_copies[1].wait()
-    local_copies[2].wait()
+                elif k < 2:
+                    copy = pltpu.make_async_copy(summed_out[k], summed_hbm.at[k], early_sem.at[k])
+                    copy.start()
+                    early_copies.append(copy)
+
+    early_copies = []
+
+    vecs[0] = jnp.zeros_like(vecs[0])
+    for row, start, ref in (
+        (0, 0, b_query), (0, 2 * cols, b_value), (1, 0, b_inner), (2, 0, b_out), (3, 0, gain_one),
+        (4, 0, shift_one), (5, 0, b_outer), (6, 0, gain_two), (7, 0, shift_two),
+    ):
+        size = ref.shape[0]
+        vecs[0, row : row + 1, start : start + size] = ref[...].astype(F32).reshape(1, size)
+    for number in (1, 5, 6, 7):
+        local_copies[number].wait()
+    pl.semaphore_wait(barrier, len(greeted))
+    send_own(0)
+    for u in (1, 2, 3):
+        vec_copies[u].start()
     build_masks()
     totals[0] = jnp.zeros_like(totals[0])
+    local_copies[0].wait()
     project(0)
     gather_turn(0)
     attend(0)
@@ -580,23 +674,31 @@
     for j in (1, 2, 3):
         gather_turn(2 + j)
         if j == 1:
-            for i in (1, 2, 3):
-                vec_copies[i].wait_recv()
+            for place in range(3):
+                pltpu.make_async_remote_copy(
+                    src_ref=vecs.at[0],
+                    dst_ref=vecs.at[place + 1],
+                    send_sem=v_send.at[place],
+                    recv_sem=v_recv.at[place],
+                    device_id=peers[1],
+                    device_id_type=MESH,
+                ).wait_recv()
         project(j)
         attend(j)
     project_out()
     norm_first()
-    local_copies[3].wait()
+    local_copies[2].wait()
     feed_in(0)
     for j in (1, 2, 3):
         gather_turn(5 + j)
         feed_in(j)
-    local_copies[4].wait()
+    local_copies[3].wait()
     feed_out(0)
     for j in (1, 2, 3):
-        gather_turn(8 + j)
+        if j > 1 or 2 not in WIDE:
+            gather_turn(8 + j - (2 in WIDE))
         feed_out(j)
-    local_copies[5].wait()
+    local_copies[4].wait()
     norm_second()
     out_copy = pltpu.make_async_copy(cot, out_hbm, local_sem.at[0])
     out_copy.start()
@@ -607,11 +709,9 @@
                 norm_first_back()
             attend_back(j)
         grad_block(k, j)
-        if k == 0:
-            feed_out_back(j)
-        elif k == 1:
+        if k == 1:
             feed_in_back(j, j == 1)
-        else:
+        elif k == 2:
             input_back(j)
         reduce_turn(turn)
     grad_in_copy = pltpu.make_async_copy(d_norm, grad_in_hbm, local_sem.at[1])
@@ -627,11 +727,20 @@
         tiny.finish(extra)
         if extra + 1 < len(everyone):
             tiny.start(extra + 1)
-    small_out[...] = totals[len(everyone)]
-
+    small_copy = pltpu.make_async_copy(totals.at[len(everyone)], small_hbm, local_sem.at[2])
+    small_copy.start()
+    last_copy = pltpu.make_async_copy(summed_out[2], summed_hbm.at[2], local_sem.at[3])
+    last_copy.start()
+
+    def settled(copies):
+        for copy in copies:
+            copy.wait_send()
+
+    for k in range(3):
+        settled(near[k])
+        for u in (2, 3):
+            pl.when(middle == 1)(lambda k=k, u=u: settled(across[k, u] + onward[k, u]))
     for item in gathered:
-        for copy in crossing[item]:
-            copy.wait_send()
         spreads[item].drain()
     for j in (1, 2, 3):
         vec_copies[j].wait_send()
@@ -643,13 +752,13 @@
     for spread in sums:
         spread.drain()
     tiny.drain()
-    out_copy.wait()
-    grad_in_copy.wait()
-
-
-def block(outer, x, cot, seg, pad, vec, own_a, own_b, own_c):
+    for copy in [out_copy, grad_in_copy, small_copy, last_copy] + early_copies:
+        copy.wait()
+
+
+def block(outer, x, cot, seg, pad, *others):
     tokens, width = x.shape
-    side = own_a.shape[0]
+    side = others[4].shape[0]
     half, cols = side // 2, side // 4
     heads = cols // HEAD_DIM
     row_count = tokens // SEQ
@@ -668,14 +777,14 @@
             jax.ShapeDtypeStruct((3, side, width), BF),
             jax.ShapeDtypeStruct((16, width), F32),
         ),
-        in_specs=[any_space, any_space, in_vmem, in_vmem, any_space, any_space, any_space, any_space],
-        out_specs=(any_space, any_space, in_vmem, in_vmem),
+        in_specs=[any_space] * 2 + [in_vmem] * 2 + [any_space] * 6 + [in_vmem] * 9,
+        out_specs=(any_space,) * 4,
         scratch_shapes=[
             vmem((3, 4, side, width), BF),
             vmem((tokens, width), BF),
             vmem((tokens, width), BF),
             vmem((row_count, SEQ, SEQ), F32),
-            vmem((4, 16, width), BF),
+            vmem((4, 8, width), F32),
             vmem((4, tokens, 3 * cols), BF),
             vmem((4, tokens, cols), BF),
             vmem((4, row_count, heads, SEQ, SEQ), BF),
@@ -683,7 +792,7 @@
             vmem((tokens, 1), F32),
             vmem((tokens, width), BF),
             vmem((4, tokens, side), BF),
-            vmem((4, tokens, side), BF),
+            vmem((max(3 * side, 4 * tokens), side), BF),
             vmem((tokens, width), F32),
             vmem((tokens, width), F32),
             vmem((tokens, width), BF),
@@ -697,7 +806,7 @@
             vmem((3, more, 2, outer_rows, width), BF),
             vmem((steps + 1, 16, width), F32),
             vmem((steps, 16, width), F32),
-            dma((3, 3, 2)), dma((3, 3, 2)), dma((3, 3, 5)), dma((3, 3, 5)), dma((3,)), dma((3,)), dma((6,)),
+            dma((3, 3, 2, 2)), dma((3, 3, 2)), dma((3, 3, 5)), dma((3, 3, 5)), dma((3,)), dma((3,)), dma((8,)), dma((2,)),
             dma((3, 4)), dma((3, 4)), dma((3, 4, 4)), dma((3, 4, 4)), dma((3, 3)), dma((3, 3)),
             dma((3, 5)), dma((3, 5)), dma((3, more)), dma((3, more)), dma((steps,)), dma((steps,)),
             pltpu.SemaphoreType.REGULAR((4,)),
@@ -706,7 +815,7 @@
             collective_id=0, has_side_effects=True, vmem_limit_bytes=67043328
         ),
         name="block",
-    )(x, cot, seg, pad, vec, own_a, own_b, own_c)
+    )(x, cot, seg, pad, *others)
 
 
 def local(
@@ -716,44 +825,90 @@
 ):
     tokens, width = block_input.shape
     cols = w_query.shape[1]
-    z = lax.axis_index("tensor")
-    own_a = jnp.concatenate([w_query.T, w_key.T, w_value.T, w_out], axis=0)
-    zero = jnp.zeros((cols,), BF)
-    vec = jnp.pad(
-        jnp.stack(
-            [
-                jnp.concatenate([b_query, zero, b_value, zero]), b_inner,
-                b_out, gain_one, shift_one, b_outer, gain_two, shift_two,
-            ]
-        ),
-        ((0, 8), (0, 0)),
-    )
     output, grad_input, summed, small = block(
         outer, block_input, cotangent, segment_ids.reshape(-1, SEQ), pad_mask.reshape(-1, SEQ),
-        vec, own_a, w_inner, w_outer,
+        w_query.T, w_key.T, w_value.T, w_out, w_inner, w_outer,
+        b_query, b_value, b_inner, b_out, gain_one, shift_one, b_outer, gain_two, shift_two,
     )
-    summed = summed.astype(F32)
-    own = lax.dynamic_slice(small, (8 + z, 0), (1, width))[0]
-    own_inner = lax.dynamic_slice(small, (12 + z, 0), (1, width))[0]
-    return (
-        output,
-        grad_input,
-        summed[2, :cols].T,
-        own[:cols],
-        summed[2, cols : 2 * cols].T,
-        summed[2, 2 * cols : 3 * cols].T,
-        own[2 * cols : 3 * cols],
-        summed[2, 3 * cols :],
-        small[0],
-        small[1],
-        small[2],
-        summed[1],
-        own_inner,
-        summed[0],
-        small[3],
-        small[4],
-        small[5],
+    outs = list(finish(output, grad_input, summed, small, cols))
+    for place in (2, 4, 5):
+        outs[place] = outs[place].T
+    return tuple(outs)
+
+
+def finish_body(
+    out_hbm, grad_in_hbm, summed_hbm, small_ref,
+    output, grad_input, g_query, gb_query, g_key, g_value, gb_value, g_out, gb_out, gg_one, gs_one,
+    g_inner, gb_inner, g_outer, gb_outer, gg_two, gs_two,
+    out_held, in_held, summed, wide, turned, flat, in_sem, out_sem,
+):
+    z = lax.axis_index("tensor")
+    cols = gb_query.shape[0]
+    reads = [pltpu.make_async_copy(summed_hbm.at[k], summed.at[k], in_sem.at[k]) for k in (0, 1, 2)]
+    reads.append(pltpu.make_async_copy(grad_in_hbm, in_held, in_sem.at[3]))
+    reads.append(pltpu.make_async_copy(out_hbm, out_held, in_sem.at[4]))
+    for copy in reads:
+        copy.start()
+    for row, ref in ((0, gb_out), (1, gg_one), (2, gs_one), (3, gb_outer), (4, gg_two), (5, gs_two)):
+        ref[...] = small_ref[row : row + 1, :].reshape(ref.shape)
+    own = small_ref[pl.ds(8 + z, 1), :]
+    gb_query[...] = own[:, :cols].reshape(gb_query.shape)
+    gb_value[...] = own[:, 2 * cols : 3 * cols].reshape(gb_value.shape)
+    gb_inner[...] = small_ref[pl.ds(12 + z, 1), :].reshape(gb_inner.shape)
+    writes = []
+
+    def write(source, target):
+        copy = pltpu.make_async_copy(source, target, out_sem.at[len(writes)])
+        copy.start()
+        writes.append(copy)
+
+    for k, target in ((0, g_outer), (1, g_inner)):
+        reads[k].wait()
+        wide[k] = summed[k].astype(F32)
+        write(wide.at[k], target)
+    reads[2].wait()
+    for part, target in enumerate((g_query, g_key, g_value)):
+        turned[part] = summed[2, part * cols : (part + 1) * cols].astype(F32)
+        write(turned.at[part], target)
+    flat[...] = summed[2, 3 * cols :].astype(F32)
+    write(flat, g_out)
+    reads[3].wait()
+    write(in_held, grad_input)
+    reads[4].wait()
+    write(out_held, output)
+    for copy in writes:
+        copy.wait()
+
+
+def finish(output, grad_input, summed, small, cols):
+    (tokens, width), side = output.shape, summed.shape[1]
+    shape = jax.ShapeDtypeStruct
+    any_space = pl.BlockSpec(memory_space=pl.ANY)
+    in_vmem = pl.BlockSpec(memory_space=pltpu.VMEM)
+    line, short, flat, big = shape((width,), F32), shape((cols,), F32), shape((cols, width), F32), shape((side, width), F32)
+    outs = (
+        (shape((tokens, width), BF), 0), (shape((tokens, width), F32), 0), (flat, 0), (short, 1), (flat, 0), (flat, 0),
+        (short, 1), (flat, 0), (line, 1), (line, 1), (line, 1), (big, 0), (line, 1), (big, 0),
+        (line, 1), (line, 1), (line, 1),
     )
+    dma = pltpu.SemaphoreType.DMA
+    return pl.pallas_call(
+        finish_body,
+        out_shape=tuple(item for item, _ in outs),
+        in_specs=[any_space, any_space, any_space, in_vmem],
+        out_specs=tuple(in_vmem if held else any_space for _, held in outs),
+        scratch_shapes=[
+            pltpu.VMEM((tokens, width), BF),
+            pltpu.VMEM((tokens, width), F32),
+            pltpu.VMEM((3, side, width), BF),
+            pltpu.VMEM((2, side, width), F32),
+            pltpu.VMEM((3, cols, width), F32),
+            pltpu.VMEM((cols, width), F32),
+            dma((5,)), dma((8,)),
+        ],
+        compiler_params=pltpu.CompilerParams(vmem_limit_bytes=67043328),
+        name="finish",
+    )(output, grad_input, summed, small)
 
 
 def solution(mesh):

time: 199 us -> 163 us (0.82)
  local copies, waits for them, and re-layouts: 15.2 us -> 0 us
  Pallas kernels: 177 us -> 162 us
  other arithmetic: 5.66 us -> 0 us
    pallas_call x1, Pallas kernels: 177 us -> 155 us  [block(): pl.pallas_call(functools.partial(block_body, outer), out_shape=(jax.Shape...]
    pallas_call x0 -> x1, Pallas kernels: none -> 6.58 us  [finish(): pl.pallas_call(finish_body, out_shape=tuple((item for item, _ in outs)),...]
    another operation x9 -> x0, local copies, waits for them, and re-layouts: 4.85 us -> none  [local(): jnp.stack([jnp.concatenate([b_query, zero, b_value, zero]), b_inner, b_ou...]
    squeeze x2 -> x0, local copies, waits for them, and re-layouts: 3.92 us -> none  [the longest x1 2.48 us: local(): summed[0]]
    concatenate x2 -> x0, other arithmetic: 3.07 us -> none  [the longest x1 2.32 us: local(): own_a = jnp.concatenate([w_query.T, w_key.T, w_value.T, w_out], axis=0)]
    slice x2 -> x0, local copies, waits for them, and re-layouts: 3 us -> none  [the longest x1 1.63 us: local(): small[5]]
    unnamed x6 -> x0, local copies, waits for them, and re-layouts: 2.83 us -> none
    convert_element_type x1 -> x0, other arithmetic: 2.6 us -> none  [local(): summed = summed.astype(F32)]
where the time goes in v1:
time: 163 us
  Pallas kernels  162 us (99%)
    pallas_call x1, Pallas kernels, block(): pl.pallas_call(functools.partial(block_body, outer), out_shape=(jax.Shape...  155 us
    pallas_call x1, Pallas kernels, finish(): pl.pallas_call(finish_body, out_shape=tuple((item for item, _ in outs)),...  6.58 us

profile of v1, /device:TPU:1, one launch (start us, length us, event | category | flops | bytes accessed | tf_op | source)
XLA Modules:
  0.0 162.7 jit_solution(5412548206878828891)
XLA Ops:
  0.7 155.2 %block.1 = (bf16[512,768]{1,0:T(8,128)(2,1)}, f32[512,768]{1,0:T(8,128)}, bf16[3,768,768]{2,1,0:T(8,128)(2,1)}, f32[16,768]{1,0:T(8,128)}) custom-call(bf16[512,768]{1,0:T(8,128)(2,1)} %x_hbm.1, bf16[512,768]{1,0:T(8,128)(2,1)} %cot_hbm.1, s32[16,128]{1,0:T(8,128)} %bitcast.11, s32[16,128]{1,0:T(8,128)} %bitcast.12, bf16[192,768]{1,0:T(8,128)(2,1)} %bitcast.8, ...), custom_call_target="tpu_custom_call" | custom-call | tf_op jit(solution)/shard_map/block/pallas_call | solution.py:772
  155.9 6.6 %finish.1 = (bf16[512,768]{1,0:T(8,128)(2,1)}, f32[512,768]{1,0:T(8,128)}, f32[192,768]{1,0:T(8,128)}, f32[192]{0:T(256)}, f32[192,768]{1,0:T(8,128)}, /*index=5...) custom-call(bf16[512,768]{1,0:T(8,128)(2,1)} %get-tuple-element.38.o, ...), custom_call_target="tpu_custom_call" | custom-call | tf_op jit(solution)/shard_map/finish/pallas_call | solution.py:895

commit v2 on v1

--- a/solution.py
+++ b/solution.py
@@ -16,7 +16,9 @@
 F32 = jnp.float32
 MESH = pl.DeviceIdType.MESH
 GROUP = 8
-WIDE = (2,)
+WIDE = ((2, 1), (2, 3))
+EARLY = ((1, 2, 3), (1,), (1,))
+MERGE_TURN = (8, 8, 12)
 
 
 def places():
@@ -167,19 +169,24 @@
     def step_one(self):
         for copy in self.one:
             copy.wait_recv()
-        for p in (0, 1):
-            self.held[self.give_two[p]] = plus(self.held[self.give_two[p]], self.from_one[p, self.inside[p]])
-            self.two[p].start()
-        for p in (0, 1):
-            self.held[self.keep_two[p]] = plus(self.held[self.keep_two[p]], self.from_one[p, self.inside_keep[p]])
+
+    def combine(self, parts, send):
+        for spans, insides in ((self.give_two, self.inside), (self.keep_two, self.inside_keep)):
+            for p in (0, 1):
+                total = self.held[spans[p]].astype(F32)
+                for part in parts:
+                    total = total + part[p, insides[p]].astype(F32)
+                self.held[spans[p]] = total.astype(BF)
+                if send and spans is self.give_two:
+                    self.two[p].start()
 
     def step_two(self, result):
         for p in (0, 1):
             self.two[p].wait_recv()
             result[p * self.eighth : (p + 1) * self.eighth] = plus(self.held[self.keep_two[p]], self.from_two[p])
 
-    def drain(self):
-        for copy in self.one + self.two:
+    def drain(self, halved):
+        for copy in self.one + (self.two if halved else []):
             copy.wait_send()
 
 
@@ -241,9 +248,9 @@
     out_hbm, grad_in_hbm, summed_hbm, small_hbm,
     weights, x_ref, cot, masks, vecs, qkv, ctx, probs, norm_one, scale_one, hidden_low, act, shared,
     acc, d_norm, d_low, d_ctx,
-    grads, from_core, from_one, from_two, zone, from_z, outer_in, totals, landing,
+    grads, from_core, from_one, from_two, zone, from_z, from_early, outer_in, totals, landing,
     gz_send, gz_recv, g_send, g_recv, v_send, v_recv, local_sem, early_sem,
-    csend, crecv, fsend, frecv, zsend, zrecv, asend, arecv, osend, orecv, ssend, srecv, credit,
+    csend, crecv, fsend, frecv, zsend, zrecv, esend, erecv, asend, arecv, osend, orecv, ssend, srecv, credit,
 ):
     dp, z, core, ax, ay, peers = places()
     others = outer_peers(dp, z, outer)
@@ -299,7 +306,7 @@
         return found
 
     for k, u in gathered:
-        spreads[k, u] = Spread(weights.at[k, u], half, g_send.at[k, u - 1], g_recv.at[k, u - 1], k in WIDE)
+        spreads[k, u] = Spread(weights.at[k, u], half, g_send.at[k, u - 1], g_recv.at[k, u - 1], (k, u) in WIDE)
     near = {k: hop(k, 0, 1, peers[1]) for k in range(3)}
     across = {(k, 2): hop(k, 0, 2, peers[3]) for k in range(3)}
     across.update({(k, 3): hop(k, 1, 3, peers[3]) for k in range(3)})
@@ -322,47 +329,46 @@
         begin(near[k])
         pl.when(middle == 1)(lambda: begin(across[k, 2]))
 
-    def line_turn(turn):
-        if turn >= len(gathered):
-            return
+    landed = {}
+    for k in range(3):
+        landed.update({(k, 1): near[k], (k, 2): across[k, 2], (k, 3): across[k, 3]})
+
+    def arrive(item):
+        for copy in landed[item]:
+            copy.wait_recv()
+
+    def ahead(turn):
         k, u = gathered[turn]
-        for copy in {1: near[k], 2: across[k, 2], 3: across[k, 3]}[u]:
-            copy.wait_recv()
-
-        def further():
-            if u == 1:
-                begin(across[k, 3])
-            else:
-                begin(onward[k, u])
-
-        pl.when(middle == 1)(further)
+
+        def forward():
+            arrive((k, u))
+            begin(across[k, 3] if u == 1 else onward[k, u])
+
+        pl.when(middle == 1)(forward)
         if u == 2 and k < 2:
             send_own(k + 1)
 
     def gather_turn(turn):
         total = len(gathered)
         if turn == 0:
-            line_turn(0)
-        if turn == 1:
-            line_turn(1)
+            ahead(0)
         if turn < total:
-            spreads[gathered[turn]].start(1 if gathered[turn][0] in WIDE else 0)
-        for lag in (1, 2):
+            item = gathered[turn]
+            pl.when(middle == 0)(lambda: arrive(item))
+            spreads[item].start(1 if item in WIDE else 0)
+        for lag in (1, 2, 3):
             if 0 <= turn - lag < total:
                 item = gathered[turn - lag]
-                if lag == 1 and item[0] in WIDE:
-                    spreads[item].finish(1)
-                    spreads[item].start(2)
-                elif item[0] not in WIDE:
-                    spreads[item].finish(lag - 1)
-                    spreads[item].start(lag)
-        line_turn(turn + 1 if turn else 9)
-        back = turn - 3
-        if 0 <= back < total and gathered[back][0] not in WIDE:
-            spreads[gathered[back]].finish(2)
-        back = turn - 2
-        if 0 <= back < total and gathered[back][0] in WIDE:
-            spreads[gathered[back]].finish(2)
+                step = lag - 1 + (item in WIDE)
+                if step < 3:
+                    spreads[item].finish(step)
+                if step < 2:
+                    spreads[item].start(step + 1)
+            if lag < 3:
+                for later in {(0, 1): (1,), (1, 1): (2,), (1, 2): (3,), (2, 2): (4,), (3, 1): (5,), (3, 2): (6,), (4, 2): (7,), (5, 2): (8,)}.get(
+                    (turn, lag), ()
+                ):
+                    ahead(later)
 
     def vector(row, slot=0):
         return vecs[slot, row : row + 1, :]
@@ -559,13 +565,41 @@
             device_id_type=MESH,
         )
         for k, j in order
-        if j
+        if j and j not in EARLY[k]
     }
+    early_slots = [(k, j) for k, j in order if j in EARLY[k]]
+    early_base = {k: early_slots.index((k, 1)) for k in range(3)}
+
+    def early_pair(k, place, item):
+        found = []
+        for p in (0, 1):
+            found.append(
+                pltpu.make_async_remote_copy(
+                    src_ref=grads.at[k % 2, item[1], mine].at[folds[item].keep_one[p]],
+                    dst_ref=from_early.at[early_base[k] + place, p],
+                    send_sem=esend.at[early_slots.index(item), p],
+                    recv_sem=erecv.at[early_base[k] + place, p],
+                    device_id=line[item[1]],
+                    device_id_type=MESH,
+                )
+            )
+        return found
+
+    early = {(k, j): early_pair(k, landing_place[j] - 1, (k, j)) for k, j in early_slots}
+
+    def merge(k, first):
+        parts = [first] if first is not None else []
+        for place in range(len(EARLY[k])):
+            for copy in early_pair(k, place, (k, 1)):
+                copy.wait_recv()
+            parts.append(from_early.at[early_base[k] + place])
+        folds[k, 0].combine(parts, True)
+
     sums = [Spread(summed_out[k], half, asend.at[k], arecv.at[k]) for k in range(3)]
     tiny = Everyone(totals, landing, ssend, srecv, everyone)
 
     def settle(k):
-        for place in range(3):
+        for place in range(len(EARLY[k]), 3):
             pltpu.make_async_remote_copy(
                 src_ref=zone.at[k, 1],
                 dst_ref=from_z.at[k, place],
@@ -575,8 +609,8 @@
                 device_id_type=MESH,
             ).wait_recv()
         summed = zone[k, 0].astype(F32)
-        for j in (1, 2, 3):
-            summed = summed + from_z[k, j - 1].astype(F32)
+        for place in range(len(EARLY[k]), 3):
+            summed = summed + from_z[k, place].astype(F32)
         for step, peer in enumerate(others):
             outer_in[k, step, 0] = summed.astype(BF)
             copy = pltpu.make_async_remote_copy(
@@ -596,7 +630,9 @@
 
     def drain(item):
         swaps[item].wait_send()
-        folds[item].drain()
+        folds[item].drain(item not in early)
+        for copy in early.get(item, ()):
+            copy.wait_send()
 
     def grad_block(k, j):
         if k == 0:
@@ -604,8 +640,8 @@
                 grads[0, j, span] = dot(act[j, :, picked], d_low[...], "TN").astype(BF)
                 if span is theirs and j:
                     swaps[k, j].start()
-            feed_out_back(j)
             if j == 0:
+                feed_out_back(j)
                 swaps[k, j].start()
         elif k == 1:
             for span, picked in ((theirs, their_cols), (mine, mine_cols)):
@@ -628,18 +664,29 @@
             if item[0] == 0:
                 pl.semaphore_signal(credit.at[item[1]], inc=1, device_id=peers["c"], device_id_type=MESH)
         if 0 <= turn - 1 < total:
-            folds[order[turn - 1]].step_one()
+            item = k, j = order[turn - 1]
+            folds[item].step_one()
+            if j == 0 and MERGE_TURN[k] == turn:
+                merge(k, from_one.at[item])
+            else:
+                folds[item].combine([from_one.at[item]], j and item not in early)
+                for copy in early.get(item, ()):
+                    copy.start()
+        for k in range(3):
+            if MERGE_TURN[k] == turn and order[turn - 1] != (k, 0):
+                merge(k, None)
         if 0 <= turn - 2 < total:
             item = order[turn - 2]
-            folds[item].step_two(zone.at[item[0], item[1]])
-            if item[1]:
+            if item[1] and item not in early:
+                folds[item].step_two(zone.at[item[0], item[1]])
                 over[item].start()
-        if turn - 3 >= 0 and (turn - 3) % 4 == 3 and turn - 3 < total:
-            settle((turn - 3) // 4)
-        for step in (0, 1, 2):
-            back = turn - 4 - step
-            if back >= 0 and back % 4 == 3 and back < total:
-                k = back // 4
+        for k in range(3):
+            if turn == MERGE_TURN[k] + 1:
+                folds[k, 0].step_two(zone.at[k, 0])
+            if turn == MERGE_TURN[k] + 2:
+                settle(k)
+            step = turn - MERGE_TURN[k] - 3
+            if 0 <= step < 3:
                 sums[k].finish(step)
                 if step < 2:
                     sums[k].start(step + 1)
@@ -685,35 +732,56 @@
                 ).wait_recv()
         project(j)
         attend(j)
+    gather_turn(6)
     project_out()
     norm_first()
+    gather_turn(7)
     local_copies[2].wait()
     feed_in(0)
-    for j in (1, 2, 3):
-        gather_turn(5 + j)
-        feed_in(j)
+    feed_in(1)
+    gather_turn(8)
+    feed_in(2)
+    feed_in(3)
+    gather_turn(9)
     local_copies[3].wait()
     feed_out(0)
-    for j in (1, 2, 3):
-        if j > 1 or 2 not in WIDE:
-            gather_turn(8 + j - (2 in WIDE))
+    feed_out(1)
+    for j in (2, 3):
+        spreads[2, j].finish(2)
         feed_out(j)
     local_copies[4].wait()
     norm_second()
     out_copy = pltpu.make_async_copy(cot, out_hbm, local_sem.at[0])
     out_copy.start()
 
-    for turn, (k, j) in enumerate(order):
-        if k == 2:
-            if j == 1:
-                norm_first_back()
-            attend_back(j)
-        grad_block(k, j)
-        if k == 1:
-            feed_in_back(j, j == 1)
-        elif k == 2:
-            input_back(j)
-        reduce_turn(turn)
+    grad_block(0, 1)
+    grad_block(0, 2)
+    reduce_turn(0)
+    grad_block(0, 3)
+    feed_out_back(1)
+    feed_out_back(2)
+    reduce_turn(1)
+    feed_out_back(3)
+    grad_block(0, 0)
+    feed_in_back(1, True)
+    reduce_turn(2)
+    for j in (2, 3, 0):
+        feed_in_back(j, False)
+    norm_first_back()
+    grad_block(1, 1)
+    reduce_turn(3)
+    for place, j in enumerate((2, 3, 0)):
+        grad_block(1, j)
+        attend_back((1, 2, 3)[place])
+        reduce_turn(4 + place)
+    attend_back(0)
+    for place, j in enumerate((1, 2, 3, 0)):
+        grad_block(2, j)
+        if place:
+            input_back(order[7 + place][1])
+        reduce_turn(7 + place)
+    input_back(0)
+    reduce_turn(11)
     grad_in_copy = pltpu.make_async_copy(d_norm, grad_in_hbm, local_sem.at[1])
     grad_in_copy.start()
     tiny.start(0)
@@ -747,7 +815,7 @@
     for item in order:
         if item[0]:
             drain(item)
-        if item[1]:
+        if item in over:
             over[item].wait_send()
     for spread in sums:
         spread.drain()
@@ -765,6 +833,7 @@
     steps = 5 + int(math.log2(outer))
     more = max(steps - 5, 1)
     outer_rows = half // 4 if outer > 1 else 16
+    early = sum(len(slots) for slots in EARLY)
     dma = pltpu.SemaphoreType.DMA
     vmem = pltpu.VMEM
     any_space = pl.BlockSpec(memory_space=pl.ANY)
@@ -803,11 +872,12 @@
             vmem((3, 4, 2, half // 8, width), BF),
             vmem((3, 4, half // 4, width), BF),
             vmem((3, 3, half // 4, width), BF),
+            vmem((early, 2, half // 4, width), BF),
             vmem((3, more, 2, outer_rows, width), BF),
             vmem((steps + 1, 16, width), F32),
             vmem((steps, 16, width), F32),
             dma((3, 3, 2, 2)), dma((3, 3, 2)), dma((3, 3, 5)), dma((3, 3, 5)), dma((3,)), dma((3,)), dma((8,)), dma((2,)),
-            dma((3, 4)), dma((3, 4)), dma((3, 4, 4)), dma((3, 4, 4)), dma((3, 3)), dma((3, 3)),
+            dma((3, 4)), dma((3, 4)), dma((3, 4, 4)), dma((3, 4, 4)), dma((3, 3)), dma((3, 3)), dma((early, 2)), dma((early, 2)),
             dma((3, 5)), dma((3, 5)), dma((3, more)), dma((3, more)), dma((steps,)), dma((steps,)),
             pltpu.SemaphoreType.REGULAR((4,)),
         ],

time: 163 us -> 160 us (0.982)
  Pallas kernels: 162 us -> 159 us
    pallas_call x1, Pallas kernels: 155 us -> 152 us  [block(): pl.pallas_call(functools.partial(block_body, outer), out_shape=(jax.Shape...]
where the time goes in v2:
time: 160 us; the launch traced here: 159 us
  Pallas kernels  159 us (99%)
    pallas_call x1, Pallas kernels, block(): pl.pallas_call(functools.partial(block_body, outer), out_shape=(jax.Shape...  152 us
    pallas_call x1, Pallas kernels, finish(): pl.pallas_call(finish_body, out_shape=tuple((item for item, _ in outs)),...  6.58 us

profile of v2, /device:TPU:1, one launch (start us, length us, event | category | flops | bytes accessed | tf_op | source)
XLA Modules:
  0.0 159.5 jit_solution(262792676447634182)
XLA Ops:
  0.7 152.0 %block.1 = (bf16[512,768]{1,0:T(8,128)(2,1)}, f32[512,768]{1,0:T(8,128)}, bf16[3,768,768]{2,1,0:T(8,128)(2,1)}, f32[16,768]{1,0:T(8,128)}) custom-call(bf16[512,768]{1,0:T(8,128)(2,1)} %x_hbm.1, bf16[512,768]{1,0:T(8,128)(2,1)} %cot_hbm.1, s32[16,128]{1,0:T(8,128)} %bitcast.11, s32[16,128]{1,0:T(8,128)} %bitcast.12, bf16[192,768]{1,0:T(8,128)(2,1)} %bitcast.8, ...), custom_call_target="tpu_custom_call" | custom-call | tf_op jit(solution)/shard_map/block/pallas_call | solution.py:841
  152.7 6.6 %finish.1 = (bf16[512,768]{1,0:T(8,128)(2,1)}, f32[512,768]{1,0:T(8,128)}, f32[192,768]{1,0:T(8,128)}, f32[192]{0:T(256)}, f32[192,768]{1,0:T(8,128)}, /*index=5...) custom-call(bf16[512,768]{1,0:T(8,128)(2,1)} %get-tuple-element.38.o, ...), custom_call_target="tpu_custom_call" | custom-call | tf_op jit(solution)/shard_map/finish/pallas_call | solution.py:965

commit v3 on v2

--- a/solution.py
+++ b/solution.py
@@ -19,6 +19,7 @@
 WIDE = ((2, 1), (2, 3))
 EARLY = ((1, 2, 3), (1,), (1,))
 MERGE_TURN = (8, 8, 12)
+SETTLE_TURN = (12, 13, 14)
 
 
 def places():
@@ -683,9 +684,10 @@
         for k in range(3):
             if turn == MERGE_TURN[k] + 1:
                 folds[k, 0].step_two(zone.at[k, 0])
-            if turn == MERGE_TURN[k] + 2:
+        for k in (2, 1, 0):
+            if turn == SETTLE_TURN[k]:
                 settle(k)
-            step = turn - MERGE_TURN[k] - 3
+            step = turn - SETTLE_TURN[k] - 1
             if 0 <= step < 3:
                 sums[k].finish(step)
                 if step < 2:
@@ -715,8 +717,8 @@
     local_copies[0].wait()
     project(0)
     gather_turn(0)
+    gather_turn(1)
     attend(0)
-    gather_turn(1)
     gather_turn(2)
     for j in (1, 2, 3):
         gather_turn(2 + j)

time: 160 us -> 154 us (0.963)
  Pallas kernels: 159 us -> 153 us
    pallas_call x1, Pallas kernels: 152 us -> 147 us  [block(): pl.pallas_call(functools.partial(block_body, outer), out_shape=(jax.Shape...]
where the time goes in v3:
time: 154 us
  Pallas kernels  153 us (99%)
    pallas_call x1, Pallas kernels, block(): pl.pallas_call(functools.partial(block_body, outer), out_shape=(jax.Shape...  147 us
    pallas_call x1, Pallas kernels, finish(): pl.pallas_call(finish_body, out_shape=tuple((item for item, _ in outs)),...  6.58 us

profile of v3, /device:TPU:1, one launch (start us, length us, event | category | flops | bytes accessed | tf_op | source)
XLA Modules:
  0.0 154.2 jit_solution(8063073648590077866)
XLA Ops:
  0.7 146.7 %block.1 = (bf16[512,768]{1,0:T(8,128)(2,1)}, f32[512,768]{1,0:T(8,128)}, bf16[3,768,768]{2,1,0:T(8,128)(2,1)}, f32[16,768]{1,0:T(8,128)}) custom-call(bf16[512,768]{1,0:T(8,128)(2,1)} %x_hbm.1, bf16[512,768]{1,0:T(8,128)(2,1)} %cot_hbm.1, s32[16,128]{1,0:T(8,128)} %bitcast.11, s32[16,128]{1,0:T(8,128)} %bitcast.12, bf16[192,768]{1,0:T(8,128)(2,1)} %bitcast.8, ...), custom_call_target="tpu_custom_call" | custom-call | tf_op jit(solution)/shard_map/block/pallas_call | solution.py:843
  147.4 6.6 %finish.1 = (bf16[512,768]{1,0:T(8,128)(2,1)}, f32[512,768]{1,0:T(8,128)}, f32[192,768]{1,0:T(8,128)}, f32[192]{0:T(256)}, f32[192,768]{1,0:T(8,128)}, /*index=5...) custom-call(bf16[512,768]{1,0:T(8,128)(2,1)} %get-tuple-element.38.o, ...), custom_call_target="tpu_custom_call" | custom-call | tf_op jit(solution)/shard_map/finish/pallas_call | solution.py:967

commit v4 on v3

--- a/solution.py
+++ b/solution.py
@@ -18,7 +18,7 @@
 GROUP = 8
 WIDE = ((2, 1), (2, 3))
 EARLY = ((1, 2, 3), (1,), (1,))
-MERGE_TURN = (8, 8, 12)
+MERGE_TURN = (7, 8, 12)
 SETTLE_TURN = (12, 13, 14)
 
 
@@ -692,7 +692,12 @@
                 sums[k].finish(step)
                 if step < 2:
                     sums[k].start(step + 1)
-                elif k < 2:
+                if k == 2 and step:
+                    part = (None, mine, theirs)[step]
+                    copy = pltpu.make_async_copy(summed_out[k].at[part], summed_hbm.at[k, part], early_sem.at[1 + step])
+                    copy.start()
+                    early_copies.append(copy)
+                elif step == 2:
                     copy = pltpu.make_async_copy(summed_out[k], summed_hbm.at[k], early_sem.at[k])
                     copy.start()
                     early_copies.append(copy)
@@ -777,30 +782,30 @@
         attend_back((1, 2, 3)[place])
         reduce_turn(4 + place)
     attend_back(0)
+
+    def tiny_turn(number):
+        if number < len(everyone):
+            tiny.finish(number)
+            if number + 1 < len(everyone):
+                tiny.start(number + 1)
+
     for place, j in enumerate((1, 2, 3, 0)):
         grad_block(2, j)
         if place:
             input_back(order[7 + place][1])
         reduce_turn(7 + place)
     input_back(0)
-    reduce_turn(11)
     grad_in_copy = pltpu.make_async_copy(d_norm, grad_in_hbm, local_sem.at[1])
     grad_in_copy.start()
+    reduce_turn(11)
     tiny.start(0)
     for extra in range(6):
-        if extra < len(everyone):
-            tiny.finish(extra)
-            if extra + 1 < len(everyone):
-                tiny.start(extra + 1)
+        tiny_turn(extra)
         reduce_turn(len(order) + extra)
     for extra in range(6, len(everyone)):
-        tiny.finish(extra)
-        if extra + 1 < len(everyone):
-            tiny.start(extra + 1)
+        tiny_turn(extra)
     small_copy = pltpu.make_async_copy(totals.at[len(everyone)], small_hbm, local_sem.at[2])
     small_copy.start()
-    last_copy = pltpu.make_async_copy(summed_out[2], summed_hbm.at[2], local_sem.at[3])
-    last_copy.start()
 
     def settled(copies):
         for copy in copies:
@@ -822,7 +827,7 @@
     for spread in sums:
         spread.drain()
     tiny.drain()
-    for copy in [out_copy, grad_in_copy, small_copy, last_copy] + early_copies:
+    for copy in [out_copy, grad_in_copy, small_copy] + early_copies:
         copy.wait()
 
 
@@ -878,7 +883,7 @@
             vmem((3, more, 2, outer_rows, width), BF),
             vmem((steps + 1, 16, width), F32),
             vmem((steps, 16, width), F32),
-            dma((3, 3, 2, 2)), dma((3, 3, 2)), dma((3, 3, 5)), dma((3, 3, 5)), dma((3,)), dma((3,)), dma((8,)), dma((2,)),
+            dma((3, 3, 2, 2)), dma((3, 3, 2)), dma((3, 3, 5)), dma((3, 3, 5)), dma((3,)), dma((3,)), dma((8,)), dma((4,)),
             dma((3, 4)), dma((3, 4)), dma((3, 4, 4)), dma((3, 4, 4)), dma((3, 3)), dma((3, 3)), dma((early, 2)), dma((early, 2)),
             dma((3, 5)), dma((3, 5)), dma((3, more)), dma((3, more)), dma((steps,)), dma((steps,)),
             pltpu.SemaphoreType.REGULAR((4,)),

time: 154 us -> 154 us (level)
  no operation moved by 1% of the time
where the time goes in v4:
time: 154 us
  Pallas kernels  153 us (99%)
    pallas_call x1, Pallas kernels, block(): pl.pallas_call(functools.partial(block_body, outer), out_shape=(jax.Shape...  146 us
    pallas_call x1, Pallas kernels, finish(): pl.pallas_call(finish_body, out_shape=tuple((item for item, _ in outs)),...  6.58 us

profile of v4, /device:TPU:1, one launch (start us, length us, event | category | flops | bytes accessed | tf_op | source)
XLA Modules:
  0.0 153.5 jit_solution(13871041241670308812)
XLA Ops:
  0.7 146.1 %block.1 = (bf16[512,768]{1,0:T(8,128)(2,1)}, f32[512,768]{1,0:T(8,128)}, bf16[3,768,768]{2,1,0:T(8,128)(2,1)}, f32[16,768]{1,0:T(8,128)}) custom-call(bf16[512,768]{1,0:T(8,128)(2,1)} %x_hbm.1, bf16[512,768]{1,0:T(8,128)(2,1)} %cot_hbm.1, s32[16,128]{1,0:T(8,128)} %bitcast.11, s32[16,128]{1,0:T(8,128)} %bitcast.12, bf16[192,768]{1,0:T(8,128)(2,1)} %bitcast.8, ...), custom_call_target="tpu_custom_call" | custom-call | tf_op jit(solution)/shard_map/block/pallas_call | solution.py:848
  146.8 6.6 %finish.1 = (bf16[512,768]{1,0:T(8,128)(2,1)}, f32[512,768]{1,0:T(8,128)}, f32[192,768]{1,0:T(8,128)}, f32[192]{0:T(256)}, f32[192,768]{1,0:T(8,128)}, /*index=5...) custom-call(bf16[512,768]{1,0:T(8,128)(2,1)} %get-tuple-element.38.o, ...), custom_call_target="tpu_custom_call" | custom-call | tf_op jit(solution)/shard_map/finish/pallas_call | solution.py:972

commit v5 on v4

--- a/solution.py
+++ b/solution.py
@@ -18,7 +18,7 @@
 GROUP = 8
 WIDE = ((2, 1), (2, 3))
 EARLY = ((1, 2, 3), (1,), (1,))
-MERGE_TURN = (7, 8, 12)
+MERGE_TURN = (6, 8, 12)
 SETTLE_TURN = (12, 13, 14)
 
 

time: 154 us -> 159 us (1.032)
  Pallas kernels: 153 us -> 158 us
    pallas_call x1, Pallas kernels: 146 us -> 151 us  [block(): pl.pallas_call(functools.partial(block_body, outer), out_shape=(jax.Shape...]
where the time goes in v5:
time: 159 us
  Pallas kernels  158 us (99%)
    pallas_call x1, Pallas kernels, block(): pl.pallas_call(functools.partial(block_body, outer), out_shape=(jax.Shape...  151 us
    pallas_call x1, Pallas kernels, finish(): pl.pallas_call(finish_body, out_shape=tuple((item for item, _ in outs)),...  6.58 us

profile of v5, /device:TPU:1, one launch (start us, length us, event | category | flops | bytes accessed | tf_op | source)
XLA Modules:
  0.0 158.6 jit_solution(5535978567478965846)
XLA Ops:
  0.7 151.1 %block.1 = (bf16[512,768]{1,0:T(8,128)(2,1)}, f32[512,768]{1,0:T(8,128)}, bf16[3,768,768]{2,1,0:T(8,128)(2,1)}, f32[16,768]{1,0:T(8,128)}) custom-call(bf16[512,768]{1,0:T(8,128)(2,1)} %x_hbm.1, bf16[512,768]{1,0:T(8,128)(2,1)} %cot_hbm.1, s32[16,128]{1,0:T(8,128)} %bitcast.11, s32[16,128]{1,0:T(8,128)} %bitcast.12, bf16[192,768]{1,0:T(8,128)(2,1)} %bitcast.8, ...), custom_call_target="tpu_custom_call" | custom-call | tf_op jit(solution)/shard_map/block/pallas_call | solution.py:848
  151.8 6.6 %finish.1 = (bf16[512,768]{1,0:T(8,128)(2,1)}, f32[512,768]{1,0:T(8,128)}, f32[192,768]{1,0:T(8,128)}, f32[192]{0:T(256)}, f32[192,768]{1,0:T(8,128)}, /*index=5...) custom-call(bf16[512,768]{1,0:T(8,128)(2,1)} %get-tuple-element.38.o, ...), custom_call_target="tpu_custom_call" | custom-call | tf_op jit(solution)/shard_map/finish/pallas_call | solution.py:972
